TPU v7x, 32 devices: a whole 2x2x4 slice. The times are simulated.
32 devices in a mesh: groups: 2 (over y), rows: 4 (over x, core), cols: 4 (over z).
Axes of the slice: x: 2, y: 2, z: 4, core: 2. Of those that a mesh axis runs over, the one named last changes fastest.
Arguments:
- pair_rep: float32 [384, 192, 128], P(('groups', 'cols'), 'rows'), parts along dimension 0, may hold values from -6 to 6
- token_mask: int32 [384], P(('groups', 'rows')), parts along dimension 0, may hold values from 0 to 1, as said below
- norm_gain: float32 [128], replicated, may hold values from 0.1 to 1.9
- norm_shift: float32 [128], replicated, may hold values from -3 to 3
- w_query: bfloat16 [128, 128], replicated, may hold values from -0.5 to 0.5
- w_keyval: bfloat16 [128, 256], replicated, may hold values from -0.5 to 0.5
- w_gate: bfloat16 [128, 128], replicated, may hold values from -0.5 to 0.5
- gate_shift: float32 [128], replicated, may hold values from -3 to 3
- w_bias: float32 [128, 4], replicated, may hold values from -12 to 12
- w_out: bfloat16 [128, 128], replicated, may hold values from -0.5 to 0.5
- out_shift: float32 [128], replicated, may hold values from -3 to 3
Outputs:
- pair_update: float32 [384, 192, 128], P(('groups', 'cols'), 'rows'), parts along dimension 0
There are 2 independent parts, one for each index of `groups`. A program takes and returns all parts, laid end to end along the dimension named above; an argument that names none is the same for every part. Nothing has to cross between parts.
Inputs may be any that keep to these rules, and one draw needn't show every extreme that they name: `token_mask`: position 0 is always a valid residue and the last position never is.
All inputs are finite; a program needn't handle non-finite values.
Results may differ from a plain program's by a relative error of at most 0.012.
The roundings to bfloat16 on the way count: a program that leaves them out, or rounds other values in their place, can miss the bound.
Values may be sent and summed in bfloat16 or wider, within the bound.
No kernel may reach another device: no remote copies, remote signals or barrier semaphores. Data moves between devices by JAX's collectives and lax.ppermute only.
A program may use at most 128 MiB of HBM per device.

v0:
```python
import jax
import jax.numpy as jnp
from jax import lax
from jax.sharding import PartitionSpec as P

HEADS = 4
HEAD_DIM = 32


def layer_norm(values, norm_gain, norm_shift):
    mean_val = jnp.mean(values, axis=-1, keepdims=True)
    centred = values - mean_val
    variance = jnp.mean(centred * centred, axis=-1, keepdims=True)
    return (centred * lax.rsqrt(variance + 1e-05) * norm_gain + norm_shift).astype(jnp.bfloat16)


def largest_divisor(count, limit):
    return max(
        (candidate for candidate in range(1, min(count, limit) + 1) if count % candidate == 0)
    )


def whole_row_layer(
    normed, token_mask, w_query, w_keyval, w_gate, gate_shift, w_bias, w_out, out_shift
):
    width = normed.shape[2]
    local_bias = jnp.dot(
        normed.astype(jnp.float32), w_bias, precision=lax.Precision.HIGHEST
    ).transpose(2, 0, 1)
    wide = lax.all_to_all(normed, "rows", split_axis=0, concat_axis=1, tiled=True)
    few_rows, token_count, _ = wide.shape
    bias_part = lax.all_gather(local_bias, "cols", axis=1, tiled=True)
    full_bias, full_mask = (
        lax.all_gather(bias_part, "rows", axis=2, tiled=True),
        lax.all_gather(token_mask.astype(jnp.float32), "rows", axis=0, tiled=True),
    )
    queries = (
        jnp.dot(wide, w_query, preferred_element_type=jnp.float32) * HEAD_DIM ** (-0.5)
    ).astype(jnp.bfloat16)
    queries = queries.reshape(few_rows, token_count, HEADS, HEAD_DIM)
    keyvals = jnp.dot(wide, w_keyval, preferred_element_type=jnp.float32).astype(jnp.bfloat16)
    keys = keyvals[..., :width].reshape(few_rows, token_count, HEADS, HEAD_DIM)
    values = keyvals[..., width:].reshape(few_rows, token_count, HEADS, HEAD_DIM)
    gates = jax.nn.sigmoid(jnp.dot(wide, w_gate, preferred_element_type=jnp.float32) + gate_shift)
    usable = full_mask > 0.5
    block_len = largest_divisor(token_count, 128)

    def one_block(block_index, gated_all):
        start = block_index * block_len
        query_block = lax.dynamic_slice_in_dim(queries, start, block_len, 1)
        bias_block = lax.dynamic_slice_in_dim(full_bias, start, block_len, 1)
        gate_block = lax.dynamic_slice_in_dim(gates, start, block_len, 1)
        scores = jnp.einsum(
            "ijhd,ikhd->hijk", query_block, keys, preferred_element_type=jnp.float32
        )
        scores = scores + bias_block[:, None]
        scores = jnp.where(usable[None, None, None, :], scores, jnp.float32(-1000000000.0))
        highest = jnp.max(scores, axis=-1, keepdims=True)
        expo = jnp.exp(scores - highest)
        total = jnp.sum(expo, axis=-1)
        weights = expo.astype(jnp.bfloat16)
        mixed = jnp.einsum("hijk,ikhd->ijhd", weights, values, preferred_element_type=jnp.float32)
        attended = mixed / total.transpose(1, 2, 0)[..., None]
        gated = (gate_block * attended.reshape(few_rows, block_len, width)).astype(jnp.bfloat16)
        return lax.dynamic_update_slice_in_dim(gated_all, gated, start, 1)

    gated_all = lax.fori_loop(
        0,
        token_count // block_len,
        one_block,
        jnp.zeros((few_rows, token_count, width), jnp.bfloat16),
    )
    gated_home = lax.all_to_all(gated_all, "rows", split_axis=1, concat_axis=0, tiled=True)
    return jnp.dot(gated_home, w_out, preferred_element_type=jnp.float32) + out_shift


def on_device(
    pair_rep,
    token_mask,
    norm_gain,
    norm_shift,
    w_query,
    w_keyval,
    w_gate,
    gate_shift,
    w_bias,
    w_out,
    out_shift,
):
    normed = layer_norm(pair_rep, norm_gain, norm_shift)
    return whole_row_layer(
        normed, token_mask, w_query, w_keyval, w_gate, gate_shift, w_bias, w_out, out_shift
    )


def solution(mesh):
    return jax.shard_map(
        on_device,
        mesh=mesh,
        in_specs=(
            P(("groups", "cols"), "rows", None),
            P(("groups", "rows")),
            P(),
            P(),
            P(),
            P(),
            P(),
            P(),
            P(),
            P(),
            P(),
        ),
        out_specs=P(("groups", "cols"), "rows", None),
        check_vma=False,
    )
```

profile of v0, /device:TPU:0, one launch (start us, length us, event | category | flops | bytes accessed | tf_op | source)
XLA Modules:
  0.0 85.9 jit_solution(3610924705760710887)
XLA Ops:
  0.0 1.7 %reduce_sum.31 = f32[48,48]{1,0:T(8,128)S(1)} reduce(f32[48,48,128]{2,1,0:T(8,128)} %param.13, f32[]{:T(128)} %constant.58.clone.1), dimensions={2}, to_apply=%region_0.0 | reduce | flops 292608 | bytes 1188868 | tf_op jit(solution)/shard_map/reduce_sum | solution.py:11
  1.8 0.7 multiply_reduce_fusion
  2.5 1.5 %add_convert_fusion = bf16[48,48,128]{2,1,0:T(8,128)(2,1)} fusion(f32[48,48,128]{2,1,0:T(8,128)S(1)} %copy-done.1, f32[128]{0:T(128)S(1)} %copy-done.8, f32[128]{0:T(128)S(1)} %copy-done.9, f32[48,48]{1,0:T(8,128)S(1)} %add_rsqrt_fusion, f32[48,48]{1,0:T(8,128)S(1)} %broadcast_multiply_fusion), kind=kLoop, calls=%fused_computation.31 | loop fusion | flops 1474560 | bytes 1788928 | tf_op jit(solution)/shard_map/convert_element_type | solution.py:14
  4.0 4.2 %all-to-all-start = ((bf16[48,48,128]{2,1,0:T(8,128)(2,1)}), bf16[48,48,128]{2,1,0:T(8,128)(2,1)S(1)}, u32[]{:S(2)}, u32[]{:S(2)}) async-start(bf16[48,48,128]{2,1,0:T(8,128)(2,1)} %add_convert_fusion), calls=%async_computation | async-start | bytes 1179648 | tf_op jit(solution)/shard_map/all_to_all | solution.py:30
  8.3 2.8 %convolution_bitcast_fusion = f32[4,48,48]{2,0,1:T(4,128)S(1)} fusion(bf16[48,48,128]{2,1,0:T(8,128)(2,1)} %add_convert_fusion, f32[128,4]{0,1:T(4,128)S(1)} %copy-done.7), kind=kOutput, calls=%fused_computation.33 | convolution fusion | flops 14155776 | bytes 628736 | tf_op jit(solution)/shard_map/dot_general | solution.py:27
  11.1 15.8 %all_gather.10 = f32[4,192,48]{2,0,1:T(4,128)S(1)} all-gather(f32[4,48,48]{2,0,1:T(4,128)S(1)} %convolution_bitcast_fusion), channel_id=1, replica_groups=mesh['groups'=2,'rows'=4,'cols'=4] {'cols'}, dimensions={1}, use_global_device_ids=true | all-gather | bytes 184320 | tf_op jit(solution)/shard_map/all_gather | solution.py:32
  27.2 0.6 dynamic-slice
  28.4 5.6 %all-reduce = f32[192]{0:T(256)S(1)} all-reduce(f32[192]{0:T(256)S(1)} %convert_dynamic-update-slice_fusion), channel_id=1, replica_groups=mesh['groups'=2,'rows'=4,'cols'=4] {'rows'}, use_global_device_ids=true, to_apply=%add | all-reduce | flops 192 | bytes 1536
  34.1 9.0 %all_gather.11 = f32[4,192,192]{1,0,2:T(4,128)S(1)} all-gather(f32[4,192,48]{1,0,2:T(4,128)S(1)} %copy.36), channel_id=1, replica_groups=mesh['groups'=2,'rows'=4,'cols'=4] {'rows'}, dimensions={2}, use_global_device_ids=true | all-gather | bytes 737280 | tf_op jit(solution)/shard_map/all_gather | solution.py:34
  43.2 0.4 convolution_convert_fusion
  43.7 0.3 fusion.39
  44.0 0.3 copy.35
  44.3 0.9 %copy.40 = bf16[12,192,4,32]{1,3,0,2:T(8,128)(2,1)} copy(bf16[12,192,4,32]{1,3,2,0:T(8,128)(2,1)S(1)} %bitcast.59) | data formatting | bytes 1179648 | tf_op jit(solution)/shard_map/while | solution.py:67
  45.2 1.2 %copy.37 = bf16[12,192,128]{1,2,0:T(8,128)(2,1)} copy(bf16[12,192,128]{2,1,0:T(8,128)(2,1)S(1)} %get-tuple-element.188) | data formatting | bytes 1179648 | tf_op jit(solution)/shard_map/slice | solution.py:43
  46.4 0.3 fusion.28
  46.7 1.2 %copy.34 = bf16[12,192,128]{1,2,0:T(8,128)(2,1)} copy(bf16[12,192,128]{2,1,0:T(8,128)(2,1)S(1)} %fusion.28) | data formatting | bytes 1179648 | tf_op jit(solution)/shard_map/convert_element_type | solution.py:39
  47.9 1.5 %fusion.27 = f32[12,192,128]{2,1,0:T(8,128)} fusion(bf16[12,192,128]{2,1,0:T(8,128)(2,1)S(1)} %bitcast.58, f32[128]{0:T(128)S(1)} %copy-done.13, bf16[128,128]{1,0:T(8,128)(2,1)S(1)} %copy-done.11), kind=kOutput, calls=%fused_computation.29 | convolution fusion | flops 76677120 | bytes 1802752 | tf_op jit(solution)/shard_map/dot_general | solution.py:44
  49.3 1.0 %broadcast_in_dim.45.clone = bf16[12,192,128]{2,0,1:T(8,128)(2,1)} broadcast(bf16[]{:T(256)} %constant.57.clone.1), dimensions={} | broadcast | bytes 589826 | tf_op jit(solution)/shard_map/broadcast_in_dim | solution.py:71
  50.3 18.9 %while.13 = (s32[]{:T(128)}, bf16[12,192,128]{2,0,1:T(8,128)(2,1)}, f32[12,192,128]{2,1,0:T(8,128)}, pred[192]{0:T(512)(128)(4,1)S(1)}, bf16[12,192,4,32]{1,3,2,...) while((s32[]{:T(128)}, bf16[12,192,128]{2,0,1:T(8,128)(2,1)}, ...), condition=%wide.region_5.6_spmd, body=%wide.region_2.5_spmd.sunk | while | flops 118112448 | bytes 19440052 | solution.py:67
  50.3 0.3 constant_dynamic-slice_fusion.13
  50.8 4.4 %fusion.59 = (f32[4,12,96]{2,1,0:T(8,128)S(1)}, bf16[4,12,96,192]{3,2,1,0:T(8,128)(2,1)}) fusion(f32[4,96,192]{2,1,0:T(8,128)S(1)} %copy.78, pred[192]{0:T(512)(128)(4,1)S(1)} %get-tuple-element.270, bf16[12,192,4,32]{1,3,0,2:T(8,128)(2,1)S(1)} %get-tuple-element.272, bf16[12,192,4,32]{1,3,2,0:T(8,128)(2,1)} %get-tuple-element.271, s32[]{:T(128)S(6)} %select_n.31), kind=kOutput, calls=%fused_computation.43.clone.1 | convolution fusion | flops 61046976 | bytes 3066052 | tf_op jit(solution)/shard_map/while/body/eval_jaxpr/sub | solution.py:59
  55.3 2.9 %fusion.60 = f32[12,96,4,32]{1,3,2,0:T(8,128)S(1)} fusion(bf16[12,192,4,32]{1,3,2,0:T(8,128)(2,1)} %get-tuple-element.274, bf16[4,12,96,192]{3,2,1,0:T(8,128)(2,1)} %get-tuple-element.241, f32[12,96,4]{1,2,0:T(4,128)S(1)} %copy.79), kind=kOutput, calls=%fused_computation.10.clone.1 | convolution fusion | flops 56770560 | bytes 2967552 | tf_op jit(solution)/shard_map/while/body/eval_jaxpr/hijk,ikhd->ijhd/dot_general | solution.py:62
  58.3 0.3 copy.77
  58.6 0.3 copy.80
  59.0 0.8 constant_dynamic-update-slice_fusion.2
  59.8 0.3 constant_dynamic-slice_fusion.13
  60.3 4.4 %fusion.59 = (f32[4,12,96]{2,1,0:T(8,128)S(1)}, bf16[4,12,96,192]{3,2,1,0:T(8,128)(2,1)}) fusion(f32[4,96,192]{2,1,0:T(8,128)S(1)} %copy.78, pred[192]{0:T(512)(128)(4,1)S(1)} %get-tuple-element.270, bf16[12,192,4,32]{1,3,0,2:T(8,128)(2,1)S(1)} %get-tuple-element.272, bf16[12,192,4,32]{1,3,2,0:T(8,128)(2,1)} %get-tuple-element.271, s32[]{:T(128)S(6)} %select_n.31), kind=kOutput, calls=%fused_computation.43.clone.1 | convolution fusion | flops 61046976 | bytes 3066052 | tf_op jit(solution)/shard_map/while/body/eval_jaxpr/sub | solution.py:59
  64.7 2.9 %fusion.60 = f32[12,96,4,32]{1,3,2,0:T(8,128)S(1)} fusion(bf16[12,192,4,32]{1,3,2,0:T(8,128)(2,1)} %get-tuple-element.274, bf16[4,12,96,192]{3,2,1,0:T(8,128)(2,1)} %get-tuple-element.241, f32[12,96,4]{1,2,0:T(4,128)S(1)} %copy.79), kind=kOutput, calls=%fused_computation.10.clone.1 | convolution fusion | flops 56770560 | bytes 2967552 | tf_op jit(solution)/shard_map/while/body/eval_jaxpr/hijk,ikhd->ijhd/dot_general | solution.py:62
  68.1 0.3 copy.80
  68.4 0.8 constant_dynamic-update-slice_fusion.2
  69.2 15.2 %all_to_all.36 = bf16[12,192,128]{2,0,1:T(8,128)(2,1)S(1)} all-to-all(bf16[12,192,128]{2,0,1:T(8,128)(2,1)} %get-tuple-element.281), channel_id=1, replica_groups=mesh['groups'=2,'rows'=4,'cols'=4] {'rows'}, dimensions={1} | all-to-all | bytes 1179648 | tf_op jit(solution)/shard_map/all_to_all | solution.py:73
  84.6 1.3 %convolution_add_fusion = f32[48,48,128]{2,1,0:T(8,128)} fusion(bf16[48,48,128]{2,1,0:T(8,128)(2,1)S(1)} %bitcast.62, f32[128]{0:T(128)S(1)} %copy-done.10, bf16[128,128]{1,0:T(8,128)(2,1)S(1)} %copy-done.5), kind=kOutput, calls=%fused_computation.23 | convolution fusion | flops 75792384 | bytes 1802752 | tf_op jit(solution)/shard_map/dot_general | solution.py:74
  (52 shorter events, 1.6 us)
Async XLA Ops:
  0.0 43.2 %copy-start = (bf16[128,256]{1,0:T(8,128)(2,1)S(1)}, bf16[128,256]{1,0:T(8,128)(2,1)}, u32[]{:S(2)}) copy-start(bf16[128,256]{1,0:T(8,128)(2,1)} %param.18) | copy-start | bytes 196612
  0.0 1.8 %copy-start.1 = (f32[48,48,128]{2,1,0:T(8,128)S(1)}, f32[48,48,128]{2,1,0:T(8,128)}, u32[]{:S(2)}) copy-start(f32[48,48,128]{2,1,0:T(8,128)} %param.13) | copy-start | bytes 3538948
  0.0 2.5 %copy-start.9 = (f32[128]{0:T(128)S(1)}, f32[128]{0:T(128)}, u32[]{:S(2)}) copy-start(f32[128]{0:T(128)} %param.15) | copy-start | bytes 1540
  0.0 2.5 %copy-start.8 = (f32[128]{0:T(128)S(1)}, f32[128]{0:T(128)}, u32[]{:S(2)}) copy-start(f32[128]{0:T(128)} %param.16) | copy-start | bytes 1540
  2.5 5.8 %copy-start.7 = (f32[128,4]{0,1:T(4,128)S(1)}, f32[128,4]{0,1:T(4,128)}, u32[]{:S(2)}) copy-start(f32[128,4]{0,1:T(4,128)} %param.21) | copy-start | bytes 6148
  4.0 39.1 %all-to-all-start = ((bf16[48,48,128]{2,1,0:T(8,128)(2,1)}), bf16[48,48,128]{2,1,0:T(8,128)(2,1)S(1)}, u32[]{:S(2)}, u32[]{:S(2)}) async-start(bf16[48,48,128]{2,1,0:T(8,128)(2,1)} %add_convert_fusion), calls=%async_computation | async-start | bytes 1179648 | tf_op jit(solution)/shard_map/all_to_all | solution.py:30
  8.3 18.9 %copy-start.14 = (u32[32]{0:T(128)S(1)}, u32[32]{0:T(128)}, u32[]{:S(2)}) copy-start(u32[32]{0:T(128)} %constant.66) | copy-start | bytes 388
  8.3 20.1 %copy-start.12 = (s32[48]{0:T(128)S(1)}, s32[48]{0:T(128)}, u32[]{:S(2)}) copy-start(s32[48]{0:T(128)} %param.14) | copy-start | bytes 580
  44.3 2.1 %copy-start.6 = (bf16[128,128]{1,0:T(8,128)(2,1)S(1)}, bf16[128,128]{1,0:T(8,128)(2,1)}, u32[]{:S(2)}) copy-start(bf16[128,128]{1,0:T(8,128)(2,1)} %param.17) | copy-start | bytes 98308
  46.4 1.5 %copy-start.11 = (bf16[128,128]{1,0:T(8,128)(2,1)S(1)}, bf16[128,128]{1,0:T(8,128)(2,1)}, u32[]{:S(2)}) copy-start(bf16[128,128]{1,0:T(8,128)(2,1)} %param.19) | copy-start | bytes 98308
  46.4 1.5 %copy-start.13 = (f32[128]{0:T(128)S(1)}, f32[128]{0:T(128)}, u32[]{:S(2)}) copy-start(f32[128]{0:T(128)} %param.20) | copy-start | bytes 1540
  47.9 2.5 %copy-start.3 = (bf16[12,192,4,32]{1,3,0,2:T(8,128)(2,1)S(1)}, bf16[12,192,4,32]{1,3,0,2:T(8,128)(2,1)}, u32[]{:S(2)}) copy-start(bf16[12,192,4,32]{1,3,0,2:T(8,128)(2,1)} %copy.40) | copy-start | bytes 1769476
  55.3 2.9 %copy-start.2 = (f32[12,192,128]{2,1,0:T(8,128)S(1)}, f32[12,192,128]{2,1,0:T(8,128)}, u32[]{:S(2)}) copy-start(f32[12,192,128]{2,1,0:T(8,128)} %get-tuple-element.269) | copy-start | bytes 3538948 | tf_op jit(solution)/shard_map/while
  58.6 1.2 %copy-start.4 = (bf16[12,192,4,32]{1,3,0,2:T(8,128)(2,1)S(1)}, bf16[12,192,4,32]{1,3,0,2:T(8,128)(2,1)}, u32[]{:S(2)}) copy-start(bf16[12,192,4,32]{1,3,0,2:T(8,128)(2,1)} %get-tuple-element.292) | copy-start | bytes 1769476 | tf_op jit(solution)/shard_map/while
  64.7 2.9 %copy-start.2 = (f32[12,192,128]{2,1,0:T(8,128)S(1)}, f32[12,192,128]{2,1,0:T(8,128)}, u32[]{:S(2)}) copy-start(f32[12,192,128]{2,1,0:T(8,128)} %get-tuple-element.269) | copy-start | bytes 3538948 | tf_op jit(solution)/shard_map/while
  68.1 1.1 %copy-start.4 = (bf16[12,192,4,32]{1,3,0,2:T(8,128)(2,1)S(1)}, bf16[12,192,4,32]{1,3,0,2:T(8,128)(2,1)}, u32[]{:S(2)}) copy-start(bf16[12,192,4,32]{1,3,0,2:T(8,128)(2,1)} %get-tuple-element.292) | copy-start | bytes 1769476 | tf_op jit(solution)/shard_map/while
  69.2 15.4 %copy-start.5 = (bf16[128,128]{1,0:T(8,128)(2,1)S(1)}, bf16[128,128]{1,0:T(8,128)(2,1)}, u32[]{:S(2)}) copy-start(bf16[128,128]{1,0:T(8,128)(2,1)} %param.22) | copy-start | bytes 98308
  69.2 15.4 %copy-start.10 = (f32[128]{0:T(128)S(1)}, f32[128]{0:T(128)}, u32[]{:S(2)}) copy-start(f32[128]{0:T(128)} %param.23) | copy-start | bytes 1540
where the time goes:
time: 86.4 us; the launch traced here: 85.9 us
  blocking collectives  45.7 us (53%)
  matrix products  21 us (24%)
  local copies, waits for them, and re-layouts  9.81 us (11%)
  other arithmetic  4.24 us (5%)
  starting transfers between devices  4.24 us (5%)
    all_gather x1, blocking collectives, whole_row_layer(): bias_part = lax.all_gather(local_bias, 'cols', axis=1, tiled=True)  15.8 us
    all_to_all x1, blocking collectives, whole_row_layer(): lax.all_to_all(gated_all, 'rows', split_axis=1, concat_axis=0, tiled=True)  15.2 us
    all_gather x1, blocking collectives, whole_row_layer(): lax.all_gather(bias_part, 'rows', axis=2, tiled=True)  9.04 us
    sub x2, matrix products, one_block(): expo = jnp.exp(scores - highest)  8.86 us
    dot_general x2, matrix products, one_block(): jnp.einsum('hijk,ikhd->ijhd', weights, values, preferred_element_type=jnp...  5.81 us
    unnamed x1, blocking collectives  5.63 us
    all_to_all x1, starting transfers between devices, whole_row_layer(): lax.all_to_all(normed, 'rows', split_axis=0, concat_axis=1, tiled=True)  4.24 us
    dot_general x1, matrix products, whole_row_layer(): jnp.dot(normed.astype(jnp.float32), w_bias, precision=lax.Precision.HIGHEST)  2.85 us
  transfers between devices with their start and end apart: 1, of which 0 were waited for; matrix products, arithmetic and copies ran while one was open for 4% of the time, Pallas kernels for 0%

commit v1 on v0

--- a/solution.py
+++ b/solution.py
@@ -5,6 +5,12 @@
 
 HEADS = 4
 HEAD_DIM = 32
+
+
+def laid_out(blocks, dim):
+    blocks = jnp.moveaxis(blocks, 0, dim)
+    shape = blocks.shape
+    return blocks.reshape(*shape[:dim], shape[dim] * shape[dim + 1], *shape[dim + 2 :])
 
 
 def layer_norm(values, norm_gain, norm_shift):
@@ -29,7 +35,19 @@
     ).transpose(2, 0, 1)
     wide = lax.all_to_all(normed, "rows", split_axis=0, concat_axis=1, tiled=True)
     few_rows, token_count, _ = wide.shape
-    bias_part = lax.all_gather(local_bias, "cols", axis=1, tiled=True)
+    length = lax.axis_size("cols")
+    pairs = [(i, (i + 1) % length) for i in range(length)]
+    back = [(b, a) for a, b in pairs]
+    lower, upper = ([], [])
+    for step in range(length - 1):
+        if step % 2 == 0:
+            lower.append(lax.ppermute(lower[-1] if lower else local_bias, "cols", pairs))
+        else:
+            upper.append(lax.ppermute(upper[-1] if upper else local_bias, "cols", back))
+    blocks = jnp.stack([*lower[::-1], local_bias, *upper])
+    shift = lax.axis_index("cols") - len(lower)
+    blocks = blocks[(jnp.arange(length) - shift) % length]
+    bias_part = laid_out(blocks, 1)
     full_bias, full_mask = (
         lax.all_gather(bias_part, "rows", axis=2, tiled=True),
         lax.all_gather(token_mask.astype(jnp.float32), "rows", axis=0, tiled=True),

time: 86.4 us -> 86.2 us (level)
  blocking collectives: 45.7 us -> 33.4 us
  waiting for transfers between devices: 0.01 us -> 6.38 us
  starting transfers between devices: 4.24 us -> 8.66 us
  local copies, waits for them, and re-layouts: 9.81 us -> 10.8 us
    all_gather x1 -> x0, blocking collectives: 15.8 us -> none  [whole_row_layer(): bias_part = lax.all_gather(local_bias, 'cols', axis=1, tiled=True)]
    ppermute x0 -> x3, waiting for transfers between devices: none -> 6.38 us  [the longest x2 6.38 us: whole_row_layer(): lax.ppermute(lower[-1] if lower else local_bias, 'cols', pairs)]
    ppermute x0 -> x3, starting transfers between devices: none -> 5.18 us  [the longest x2 3.14 us: whole_row_layer(): lax.ppermute(lower[-1] if lower else local_bias, 'cols', pairs)]
    unnamed x1, blocking collectives: 5.63 us -> 9.47 us
  transfers between devices with their start and end apart: 1 -> 4, of which waited for: 0 -> 1; matrix products, arithmetic and copies ran while one was open for 4% -> 2% of each run, Pallas kernels for 0% -> 0%
where the time goes in v1:
time: 86.2 us; the launch traced here: 85.7 us
  blocking collectives  33.4 us (39%)
  matrix products  21.1 us (24%)
  local copies, waits for them, and re-layouts  10.8 us (13%)
  starting transfers between devices  8.66 us (10%)
  waiting for transfers between devices  6.38 us (7%)
  other arithmetic  4.36 us (5%)
  between operations  0.93 us (1%)
    all_to_all x1, blocking collectives, whole_row_layer(): lax.all_to_all(gated_all, 'rows', split_axis=1, concat_axis=0, tiled=True)  15.2 us
    unnamed x1, blocking collectives  9.47 us
    sub x2, matrix products, one_block(): expo = jnp.exp(scores - highest)  8.87 us
    all_gather x1, blocking collectives, whole_row_layer(): lax.all_gather(bias_part, 'rows', axis=2, tiled=True)  8.74 us
    ppermute x2, waiting for transfers between devices, whole_row_layer(): lax.ppermute(lower[-1] if lower else local_bias, 'cols', pairs)  6.38 us
    dot_general x2, matrix products, one_block(): jnp.einsum('hijk,ikhd->ijhd', weights, values, preferred_element_type=jnp...  5.81 us
    all_to_all x1, starting transfers between devices, whole_row_layer(): lax.all_to_all(normed, 'rows', split_axis=0, concat_axis=1, tiled=True)  3.48 us
    ppermute x2, starting transfers between devices, whole_row_layer(): lax.ppermute(lower[-1] if lower else local_bias, 'cols', pairs)  3.14 us
  transfers between devices with their start and end apart: 4, of which 1 were waited for; matrix products, arithmetic and copies ran while one was open for 2% of the time, Pallas kernels for 0%

profile of v1, /device:TPU:0, one launch (start us, length us, event | category | flops | bytes accessed | tf_op | source)
XLA Modules:
  0.0 85.7 jit_solution(9065879832374633326)
XLA Ops:
  0.0 1.7 %reduce_sum.31 = f32[48,48]{1,0:T(8,128)S(1)} reduce(f32[48,48,128]{2,1,0:T(8,128)} %param.13, f32[]{:T(128)} %constant.77.clone.1), dimensions={2}, to_apply=%region_0.0 | reduce | flops 292608 | bytes 1188868 | tf_op jit(solution)/shard_map/reduce_sum | solution.py:17
  1.8 0.7 multiply_reduce_fusion
  2.5 1.5 %add_convert_fusion = bf16[48,48,128]{2,1,0:T(8,128)(2,1)} fusion(f32[48,48,128]{2,1,0:T(8,128)S(1)} %copy-done.1, f32[128]{0:T(128)S(1)} %copy-done.8, f32[128]{0:T(128)S(1)} %copy-done.9, f32[48,48]{1,0:T(8,128)S(1)} %add_rsqrt_fusion, f32[48,48]{1,0:T(8,128)S(1)} %broadcast_multiply_fusion), kind=kLoop, calls=%fused_computation.32 | loop fusion | flops 1474560 | bytes 1788928 | tf_op jit(solution)/shard_map/convert_element_type | solution.py:20
  4.0 2.9 %fusion.33 = f32[48,48,4]{1,2,0:T(4,128)S(1)} fusion(bf16[48,48,128]{2,1,0:T(8,128)(2,1)} %add_convert_fusion, f32[128,4]{0,1:T(4,128)S(1)} %copy-done.7), kind=kOutput, calls=%fused_computation.45 | convolution fusion | flops 14155776 | bytes 628736 | tf_op jit(solution)/shard_map/dot_general | solution.py:33
  6.9 3.1 %collective-permute-start = (f32[4,48,48]{2,0,1:T(4,128)S(1)}, f32[4,48,48]{2,0,1:T(4,128)S(1)}, u32[]{:S(2)}, u32[]{:S(2)}) collective-permute-start(f32[4,48,48]{2,0,1:T(4,128)S(1)} %bitcast.74), channel_id=1, source_target_pairs={{0,1},{1,2},{2,3},{3,0},{4,5},{5,6},{6,7},{7,4},{8,9},{9,10},{10,1... | collective-permute-start | bytes 110600 | tf_op jit(solution)/shard_map/ppermute | solution.py:44
  10.0 2.0 %collective-permute-start.2 = (f32[4,48,48]{2,0,1:T(4,128)S(1)}, f32[4,48,48]{2,0,1:T(4,128)S(1)}, u32[]{:S(2)}, u32[]{:S(2)}) collective-permute-start(f32[4,48,48]{2,0,1:T(4,128)S(1)} %bitcast.75), channel_id=1, source_target_pairs={{1,0},{2,1},{3,2},{0,3},{5,4},{6,5},{7,6},{4,7},{9,8},{10,9},{11,1... | collective-permute-start | bytes 110600 | tf_op jit(solution)/shard_map/ppermute | solution.py:46
  12.0 3.5 %all-to-all-start = ((bf16[48,48,128]{2,1,0:T(8,128)(2,1)}), bf16[48,48,128]{2,1,0:T(8,128)(2,1)S(1)}, u32[]{:S(2)}, u32[]{:S(2)}) async-start(bf16[48,48,128]{2,1,0:T(8,128)(2,1)} %add_convert_fusion), calls=%async_computation | async-start | bytes 1179648 | tf_op jit(solution)/shard_map/all_to_all | solution.py:36
  15.5 0.7 dynamic-slice
  17.0 9.5 %all-reduce = f32[192]{0:T(256)S(1)} all-reduce(f32[192]{0:T(256)S(1)} %convert_dynamic-update-slice_fusion), channel_id=1, replica_groups=mesh['groups'=2,'rows'=4,'cols'=4] {'rows'}, use_global_device_ids=true, to_apply=%add | all-reduce | flops 192 | bytes 1536
  26.6 6.4 %collective-permute-done.1 = f32[4,48,48]{2,0,1:T(4,128)S(1)} collective-permute-done((f32[4,48,48]{2,0,1:T(4,128)S(1)}, f32[4,48,48]{2,0,1:T(4,128)S(1)}, u32[]{:S(2)}, u32[]{:S(2)}) %collective-permute-start.1) | collective-permute-done | bytes 36896 | tf_op jit(solution)/shard_map/ppermute | solution.py:44
  33.1 0.8 gather_fusion
  34.1 8.7 %all_gather.7 = f32[4,192,192]{1,0,2:T(4,128)S(1)} all-gather(f32[4,192,48]{1,0,2:T(4,128)S(1)} %copy.36), channel_id=1, replica_groups=mesh['groups'=2,'rows'=4,'cols'=4] {'rows'}, dimensions={2}, use_global_device_ids=true | all-gather | bytes 737280 | tf_op jit(solution)/shard_map/all_gather | solution.py:52
  42.9 0.4 convolution_convert_fusion
  43.3 0.3 fusion.42
  43.7 0.3 copy.35
  44.0 1.0 %copy.40 = bf16[12,192,4,32]{1,3,0,2:T(8,128)(2,1)} copy(bf16[12,192,4,32]{1,3,2,0:T(8,128)(2,1)S(1)} %bitcast.68) | data formatting | bytes 1179648 | tf_op jit(solution)/shard_map/while | solution.py:85
  44.9 1.2 %copy.37 = bf16[12,192,128]{1,2,0:T(8,128)(2,1)} copy(bf16[12,192,128]{2,1,0:T(8,128)(2,1)S(1)} %get-tuple-element.188) | data formatting | bytes 1179648 | tf_op jit(solution)/shard_map/slice | solution.py:61
  46.1 0.3 fusion.28
  46.4 1.2 %copy.34 = bf16[12,192,128]{1,2,0:T(8,128)(2,1)} copy(bf16[12,192,128]{2,1,0:T(8,128)(2,1)S(1)} %fusion.28) | data formatting | bytes 1179648 | tf_op jit(solution)/shard_map/convert_element_type | solution.py:57
  47.6 1.5 %fusion.27 = f32[12,192,128]{2,1,0:T(8,128)} fusion(bf16[12,192,128]{2,1,0:T(8,128)(2,1)S(1)} %bitcast.67, f32[128]{0:T(128)S(1)} %copy-done.13, bf16[128,128]{1,0:T(8,128)(2,1)S(1)} %copy-done.11), kind=kOutput, calls=%fused_computation.30 | convolution fusion | flops 76677120 | bytes 1802752 | tf_op jit(solution)/shard_map/dot_general | solution.py:62
  49.1 1.0 %broadcast_in_dim.46.clone = bf16[12,192,128]{2,0,1:T(8,128)(2,1)} broadcast(bf16[]{:T(256)} %constant.76.clone.1), dimensions={} | broadcast | bytes 589826 | tf_op jit(solution)/shard_map/broadcast_in_dim | solution.py:89
  50.1 18.9 %while.13 = (s32[]{:T(128)}, bf16[12,192,128]{2,0,1:T(8,128)(2,1)}, f32[12,192,128]{2,1,0:T(8,128)}, pred[192]{0:T(512)(128)(4,1)S(1)}, bf16[12,192,4,32]{1,3,2,...) while((s32[]{:T(128)}, bf16[12,192,128]{2,0,1:T(8,128)(2,1)}, ...), condition=%wide.region_5.6_spmd, body=%wide.region_2.5_spmd.sunk | while | flops 118112448 | bytes 19440052 | solution.py:85
  50.6 4.4 %fusion.62 = (f32[4,12,96]{2,1,0:T(8,128)S(1)}, bf16[4,12,96,192]{3,2,1,0:T(8,128)(2,1)}) fusion(f32[4,96,192]{2,1,0:T(8,128)S(1)} %copy.78, pred[192]{0:T(512)(128)(4,1)S(1)} %get-tuple-element.270, bf16[12,192,4,32]{1,3,0,2:T(8,128)(2,1)S(1)} %get-tuple-element.272, bf16[12,192,4,32]{1,3,2,0:T(8,128)(2,1)} %get-tuple-element.271, s32[]{:T(128)S(6)} %select_n.65), kind=kOutput, calls=%fused_computation.52.clone.1 | convolution fusion | flops 61046976 | bytes 3066052 | tf_op jit(solution)/shard_map/while/body/eval_jaxpr/sub | solution.py:77
  55.0 2.9 %fusion.63 = f32[12,96,4,32]{1,3,2,0:T(8,128)S(1)} fusion(bf16[12,192,4,32]{1,3,2,0:T(8,128)(2,1)} %get-tuple-element.274, bf16[4,12,96,192]{3,2,1,0:T(8,128)(2,1)} %get-tuple-element.241, f32[12,96,4]{1,2,0:T(4,128)S(1)} %copy.79), kind=kOutput, calls=%fused_computation.11.clone.1 | convolution fusion | flops 56770560 | bytes 2967552 | tf_op jit(solution)/shard_map/while/body/eval_jaxpr/hijk,ikhd->ijhd/dot_general | solution.py:80
  58.4 0.3 copy.80
  58.7 0.8 constant_dynamic-update-slice_fusion.2
  60.0 4.4 %fusion.62 = (f32[4,12,96]{2,1,0:T(8,128)S(1)}, bf16[4,12,96,192]{3,2,1,0:T(8,128)(2,1)}) fusion(f32[4,96,192]{2,1,0:T(8,128)S(1)} %copy.78, pred[192]{0:T(512)(128)(4,1)S(1)} %get-tuple-element.270, bf16[12,192,4,32]{1,3,0,2:T(8,128)(2,1)S(1)} %get-tuple-element.272, bf16[12,192,4,32]{1,3,2,0:T(8,128)(2,1)} %get-tuple-element.271, s32[]{:T(128)S(6)} %select_n.65), kind=kOutput, calls=%fused_computation.52.clone.1 | convolution fusion | flops 61046976 | bytes 3066052 | tf_op jit(solution)/shard_map/while/body/eval_jaxpr/sub | solution.py:77
  64.5 2.9 %fusion.63 = f32[12,96,4,32]{1,3,2,0:T(8,128)S(1)} fusion(bf16[12,192,4,32]{1,3,2,0:T(8,128)(2,1)} %get-tuple-element.274, bf16[4,12,96,192]{3,2,1,0:T(8,128)(2,1)} %get-tuple-element.241, f32[12,96,4]{1,2,0:T(4,128)S(1)} %copy.79), kind=kOutput, calls=%fused_computation.11.clone.1 | convolution fusion | flops 56770560 | bytes 2967552 | tf_op jit(solution)/shard_map/while/body/eval_jaxpr/hijk,ikhd->ijhd/dot_general | solution.py:80
  67.8 0.3 copy.80
  68.2 0.8 constant_dynamic-update-slice_fusion.2
  69.0 15.2 %all_to_all.36 = bf16[12,192,128]{2,0,1:T(8,128)(2,1)S(1)} all-to-all(bf16[12,192,128]{2,0,1:T(8,128)(2,1)} %get-tuple-element.281), channel_id=1, replica_groups=mesh['groups'=2,'rows'=4,'cols'=4] {'rows'}, dimensions={1} | all-to-all | bytes 1179648 | tf_op jit(solution)/shard_map/all_to_all | solution.py:91
  84.4 1.3 %convolution_add_fusion = f32[48,48,128]{2,1,0:T(8,128)} fusion(bf16[48,48,128]{2,1,0:T(8,128)(2,1)S(1)} %bitcast.71, f32[128]{0:T(128)S(1)} %copy-done.10, bf16[128,128]{1,0:T(8,128)(2,1)S(1)} %copy-done.5), kind=kOutput, calls=%fused_computation.24 | convolution fusion | flops 75792384 | bytes 1802752 | tf_op jit(solution)/shard_map/dot_general | solution.py:92
  (61 shorter events, 2.6 us)
Async XLA Ops:
  0.0 42.9 %copy-start = (bf16[128,256]{1,0:T(8,128)(2,1)S(1)}, bf16[128,256]{1,0:T(8,128)(2,1)}, u32[]{:S(2)}) copy-start(bf16[128,256]{1,0:T(8,128)(2,1)} %param.18) | copy-start | bytes 196612
  0.0 1.8 %copy-start.1 = (f32[48,48,128]{2,1,0:T(8,128)S(1)}, f32[48,48,128]{2,1,0:T(8,128)}, u32[]{:S(2)}) copy-start(f32[48,48,128]{2,1,0:T(8,128)} %param.13) | copy-start | bytes 3538948
  0.0 2.5 %copy-start.9 = (f32[128]{0:T(128)S(1)}, f32[128]{0:T(128)}, u32[]{:S(2)}) copy-start(f32[128]{0:T(128)} %param.15) | copy-start | bytes 1540
  0.0 2.5 %copy-start.8 = (f32[128]{0:T(128)S(1)}, f32[128]{0:T(128)}, u32[]{:S(2)}) copy-start(f32[128]{0:T(128)} %param.16) | copy-start | bytes 1540
  2.5 1.6 %copy-start.7 = (f32[128,4]{0,1:T(4,128)S(1)}, f32[128,4]{0,1:T(4,128)}, u32[]{:S(2)}) copy-start(f32[128,4]{0,1:T(4,128)} %param.21) | copy-start | bytes 6148
  4.0 11.5 %copy-start.14 = (u32[32]{0:T(128)S(1)}, u32[32]{0:T(128)}, u32[]{:S(2)}) copy-start(u32[32]{0:T(128)} %constant.89) | copy-start | bytes 388
  4.0 12.8 %copy-start.12 = (s32[48]{0:T(128)S(1)}, s32[48]{0:T(128)}, u32[]{:S(2)}) copy-start(s32[48]{0:T(128)} %param.14) | copy-start | bytes 580
  6.9 19.6 %collective-permute-start = (f32[4,48,48]{2,0,1:T(4,128)S(1)}, f32[4,48,48]{2,0,1:T(4,128)S(1)}, u32[]{:S(2)}, u32[]{:S(2)}) collective-permute-start(f32[4,48,48]{2,0,1:T(4,128)S(1)} %bitcast.74), channel_id=1, source_target_pairs={{0,1},{1,2},{2,3},{3,0},{4,5},{5,6},{6,7},{7,4},{8,9},{9,10},{10,1... | collective-permute-start | bytes 110600 | tf_op jit(solution)/shard_map/ppermute | solution.py:44
  10.0 16.6 %collective-permute-start.2 = (f32[4,48,48]{2,0,1:T(4,128)S(1)}, f32[4,48,48]{2,0,1:T(4,128)S(1)}, u32[]{:S(2)}, u32[]{:S(2)}) collective-permute-start(f32[4,48,48]{2,0,1:T(4,128)S(1)} %bitcast.75), channel_id=1, source_target_pairs={{1,0},{2,1},{3,2},{0,3},{5,4},{6,5},{7,6},{4,7},{9,8},{10,9},{11,1... | collective-permute-start | bytes 110600 | tf_op jit(solution)/shard_map/ppermute | solution.py:46
  12.0 30.8 %all-to-all-start = ((bf16[48,48,128]{2,1,0:T(8,128)(2,1)}), bf16[48,48,128]{2,1,0:T(8,128)(2,1)S(1)}, u32[]{:S(2)}, u32[]{:S(2)}) async-start(bf16[48,48,128]{2,1,0:T(8,128)(2,1)} %add_convert_fusion), calls=%async_computation | async-start | bytes 1179648 | tf_op jit(solution)/shard_map/all_to_all | solution.py:36
  26.5 6.5 %collective-permute-start.1 = (f32[4,48,48]{2,0,1:T(4,128)S(1)}, f32[4,48,48]{2,0,1:T(4,128)S(1)}, u32[]{:S(2)}, u32[]{:S(2)}) collective-permute-start(f32[4,48,48]{2,0,1:T(4,128)S(1)} %collective-permute-done), channel_id=1, source_target_pairs={{0,1},{1,2},{2,3},{3,0},{4,5},{5,6},{6,7},{7,4},{8,9},{9,10},{10,1... | collective-permute-start | bytes 110600 | tf_op jit(solution)/shard_map/ppermute | solution.py:44
  43.9 2.2 %copy-start.6 = (bf16[128,128]{1,0:T(8,128)(2,1)S(1)}, bf16[128,128]{1,0:T(8,128)(2,1)}, u32[]{:S(2)}) copy-start(bf16[128,128]{1,0:T(8,128)(2,1)} %param.17) | copy-start | bytes 98308
  46.1 1.5 %copy-start.11 = (bf16[128,128]{1,0:T(8,128)(2,1)S(1)}, bf16[128,128]{1,0:T(8,128)(2,1)}, u32[]{:S(2)}) copy-start(bf16[128,128]{1,0:T(8,128)(2,1)} %param.19) | copy-start | bytes 98308
  46.1 1.5 %copy-start.13 = (f32[128]{0:T(128)S(1)}, f32[128]{0:T(128)}, u32[]{:S(2)}) copy-start(f32[128]{0:T(128)} %param.20) | copy-start | bytes 1540
  47.6 2.5 %copy-start.3 = (bf16[12,192,4,32]{1,3,0,2:T(8,128)(2,1)S(1)}, bf16[12,192,4,32]{1,3,0,2:T(8,128)(2,1)}, u32[]{:S(2)}) copy-start(bf16[12,192,4,32]{1,3,0,2:T(8,128)(2,1)} %copy.40) | copy-start | bytes 1769476
  55.0 2.9 %copy-start.2 = (f32[12,192,128]{2,1,0:T(8,128)S(1)}, f32[12,192,128]{2,1,0:T(8,128)}, u32[]{:S(2)}) copy-start(f32[12,192,128]{2,1,0:T(8,128)} %get-tuple-element.269) | copy-start | bytes 3538948 | tf_op jit(solution)/shard_map/while
  58.4 1.2 %copy-start.4 = (bf16[12,192,4,32]{1,3,0,2:T(8,128)(2,1)S(1)}, bf16[12,192,4,32]{1,3,0,2:T(8,128)(2,1)}, u32[]{:S(2)}) copy-start(bf16[12,192,4,32]{1,3,0,2:T(8,128)(2,1)} %get-tuple-element.292) | copy-start | bytes 1769476 | tf_op jit(solution)/shard_map/while
  64.5 2.9 %copy-start.2 = (f32[12,192,128]{2,1,0:T(8,128)S(1)}, f32[12,192,128]{2,1,0:T(8,128)}, u32[]{:S(2)}) copy-start(f32[12,192,128]{2,1,0:T(8,128)} %get-tuple-element.269) | copy-start | bytes 3538948 | tf_op jit(solution)/shard_map/while
  67.8 1.2 %copy-start.4 = (bf16[12,192,4,32]{1,3,0,2:T(8,128)(2,1)S(1)}, bf16[12,192,4,32]{1,3,0,2:T(8,128)(2,1)}, u32[]{:S(2)}) copy-start(bf16[12,192,4,32]{1,3,0,2:T(8,128)(2,1)} %get-tuple-element.292) | copy-start | bytes 1769476 | tf_op jit(solution)/shard_map/while
  69.0 15.4 %copy-start.5 = (bf16[128,128]{1,0:T(8,128)(2,1)S(1)}, bf16[128,128]{1,0:T(8,128)(2,1)}, u32[]{:S(2)}) copy-start(bf16[128,128]{1,0:T(8,128)(2,1)} %param.22) | copy-start | bytes 98308
  69.0 15.4 %copy-start.10 = (f32[128]{0:T(128)S(1)}, f32[128]{0:T(128)}, u32[]{:S(2)}) copy-start(f32[128]{0:T(128)} %param.23) | copy-start | bytes 1540
